TPU v7x, 32 devices: a whole 2x2x4 slice. The times are simulated.
32 devices in a mesh: recv: 4 (over x, core), send: 8 (over z, y).
Axes of the slice: x: 2, y: 2, z: 4, core: 2. Of those that a mesh axis runs over, the one named last changes fastest.
Arguments:
- latent: float32 [4096, 512], P(('recv', 'send')), may hold values from -6 to 6
- edge_feat: float32 [32768, 512], P(('recv', 'send')), may hold values from -6 to 6
- senders: int32 [32768], P(('recv', 'send')), may hold values from 0 to 4095, as said below
- receivers: int32 [32768], P(('recv', 'send')), may hold values from 0 to 4095, as said below
- live_blocks: int32 [32], P(('recv', 'send')), may hold values from 1 to 8, as said below
- cotangent: float32 [32768, 512], P(('recv', 'send')), may hold values from -6 to 6
- w_first: float32 [1536, 512], replicated, may hold values from -0.15625 to 0.15625
- first_bias: float32 [512], replicated, may hold values from -3 to 3
- w_second: float32 [512, 512], replicated, may hold values from -0.25 to 0.25
- second_bias: float32 [512], replicated, may hold values from -3 to 3
- norm_gain: float32 [512], replicated, may hold values from 0.1 to 1.9
Outputs:
- edge_grad: float32 [32768, 512], P(('recv', 'send'))
- sender_grad: float32 [4096, 512], P(('recv', 'send'))
- receiver_grad: float32 [4096, 512], P(('recv', 'send'))
- first_weight_grad: float32 [1536, 512], replicated
- second_weight_grad: float32 [512, 512], replicated
- bias_grads: float32 [4, 512], replicated
Inputs may be any that keep to these rules, and one draw needn't show every extreme that they name: `receivers`: slot e lies in tile t = e // 1024; with i = t // (devices along send), its receiver r has (r // 128) // (devices along send) = i. The first two slots of every tile name the last and the first node of that receiver block. `senders`: slot e lies in tile t = e // 1024; with j = t mod (devices along send), its sender s has (s // 128) mod (devices along send) = j. The first two slots of every tile name the last and the first node of that sender block. Tile t's first 128 * live_blocks[t] slots hold edges; its other slots are padding whose cotangent is ignored. Some tile is full in every draw.
All inputs are finite; a program needn't handle non-finite values.
Results may differ from a plain program's by a relative error of at most 0.0001.
Values sent between devices are 32-bit elements; how exact they have to be, the bound alone decides.
A program may use at most 128 MiB of HBM per device.

v0:
```python
import math
import jax
import jax.numpy as jnp
from jax import lax
from jax.sharding import PartitionSpec as P

norm_eps = 1e-05
block_rows = 128


def exact_dot(left, right):
    return jnp.dot(left, right, precision=lax.Precision.HIGHEST, preferred_element_type=jnp.float32)


def outer_sum(left, right):
    return lax.dot_general(
        left,
        right,
        (((0,), (0,)), ((), ())),
        precision=lax.Precision.HIGHEST,
        preferred_element_type=jnp.float32,
    )


def trans_dot(left, right):
    return lax.dot_general(
        left,
        right,
        (((1,), (1,)), ((), ())),
        precision=lax.Precision.HIGHEST,
        preferred_element_type=jnp.float32,
    )


def shards(
    latent,
    edge_feat,
    senders,
    receivers,
    live_blocks,
    cotangent,
    w_first,
    first_bias,
    w_second,
    second_bias,
    norm_gain,
):
    model_width = latent.shape[1]
    node_rows = latent.shape[0]
    slot_count = edge_feat.shape[0]
    recv_count = lax.axis_size("recv")
    send_count = lax.axis_size("send")
    recv_index = lax.axis_index("recv")
    recv_local = receivers - recv_index * (send_count * node_rows)
    piece_index = senders // node_rows
    send_local = piece_index // send_count * node_rows + senders % node_rows
    live_limit = block_rows * live_blocks[0]
    sender_table = lax.all_gather(latent, "recv", axis=0, tiled=True)
    receiver_table = lax.all_gather(latent, "send", axis=0, tiled=True)
    first_rows = 3 * model_width

    def block_work(accs, edge_rows, grad_rows, sender_rows, recv_ids):
        first_grad, second_grad, hidden_bias, outer_bias, gain_grad, offset_grad, receiver_acc = (
            accs
        )
        receiver_rows = jnp.take(receiver_table, recv_ids, axis=0)
        joined = jnp.concatenate([edge_rows, sender_rows, receiver_rows], axis=1)
        hidden = exact_dot(joined, w_first) + first_bias
        sigmoid_hidden = jax.nn.sigmoid(hidden)
        active = hidden * sigmoid_hidden
        output = exact_dot(active, w_second) + second_bias
        centred = output - jnp.mean(output, axis=1, keepdims=True)
        inv_std = lax.rsqrt(jnp.mean(centred * centred, axis=1, keepdims=True) + norm_eps)
        normed = centred * inv_std
        scaled = grad_rows * norm_gain
        norm_grad = inv_std * (
            scaled
            - jnp.mean(scaled, axis=1, keepdims=True)
            - normed * jnp.mean(scaled * normed, axis=1, keepdims=True)
        )
        hidden_grad = (
            trans_dot(norm_grad, w_second)
            * sigmoid_hidden
            * (1.0 + hidden * (1.0 - sigmoid_hidden))
        )
        first_grad = first_grad + outer_sum(joined, hidden_grad)
        second_grad = second_grad + outer_sum(active, norm_grad)
        hidden_bias = hidden_bias + jnp.sum(hidden_grad, axis=0)
        outer_bias = outer_bias + jnp.sum(norm_grad, axis=0)
        gain_grad = gain_grad + jnp.sum(grad_rows * normed, axis=0)
        offset_grad = offset_grad + jnp.sum(grad_rows, axis=0)
        joined_grad = trans_dot(hidden_grad, w_first)
        edge_part = joined_grad[:, :model_width]
        sender_part = joined_grad[:, model_width : 2 * model_width]
        receiver_acc = receiver_acc.at[recv_ids].add(joined_grad[:, 2 * model_width :])
        accs = (
            first_grad,
            second_grad,
            hidden_bias,
            outer_bias,
            gain_grad,
            offset_grad,
            receiver_acc,
        )
        return (accs, grad_rows + edge_part, sender_part)

    def local_block(offset):
        edge_rows = lax.dynamic_slice_in_dim(edge_feat, offset, block_rows, 0)
        position = offset + jnp.arange(block_rows, dtype=jnp.int32)
        live_rows = (position < live_limit).astype(jnp.float32)[:, None]
        grad_rows = lax.dynamic_slice_in_dim(cotangent, offset, block_rows, 0) * live_rows
        send_ids = lax.dynamic_slice_in_dim(send_local, offset, block_rows, 0)
        recv_ids = lax.dynamic_slice_in_dim(recv_local, offset, block_rows, 0)
        sender_rows = jnp.take(sender_table, send_ids, axis=0)
        return (edge_rows, grad_rows, send_ids, recv_ids, sender_rows)

    feature_zeros = jnp.zeros((model_width,), jnp.float32)
    accs = (
        jnp.zeros((first_rows, model_width), jnp.float32),
        jnp.zeros((model_width, model_width), jnp.float32),
        feature_zeros,
        feature_zeros,
        feature_zeros,
        feature_zeros,
        jnp.zeros(receiver_table.shape, jnp.float32),
    )
    sender_acc = jnp.zeros(sender_table.shape, jnp.float32)
    edge_out = jnp.zeros(edge_feat.shape, jnp.float32)

    def own_step(block, carried):
        accs_now, sender_now, edge_now = carried
        offset = block * block_rows
        edge_rows, grad_rows, send_ids, recv_ids, sender_rows = local_block(offset)
        accs_now, edge_block, sender_block = block_work(
            accs_now, edge_rows, grad_rows, sender_rows, recv_ids
        )
        sender_now = sender_now.at[send_ids].add(sender_block)
        edge_now = lax.dynamic_update_slice_in_dim(edge_now, edge_block, offset, 0)
        return (accs_now, sender_now, edge_now)

    accs, sender_acc, edge_out = lax.fori_loop(
        0, live_blocks[0], own_step, (accs, sender_acc, edge_out)
    )
    first_grad, second_grad, hidden_bias, outer_bias, gain_grad, offset_grad, receiver_acc = accs
    sender_grad = lax.psum_scatter(sender_acc, "recv", scatter_dimension=0, tiled=True)
    receiver_grad = lax.psum_scatter(receiver_acc, "send", scatter_dimension=0, tiled=True)
    small_grads = jnp.stack([hidden_bias, outer_bias, gain_grad, offset_grad])
    first_total, second_total, small_total = lax.psum(
        (first_grad, second_grad, small_grads), ("recv", "send")
    )
    factor = 1.0 / math.sqrt(slot_count * recv_count * send_count)
    return (
        edge_out,
        sender_grad,
        receiver_grad,
        first_total * factor,
        second_total * factor,
        small_total * factor,
    )


def solution(mesh):
    return jax.shard_map(
        shards,
        mesh=mesh,
        in_specs=(
            P(("recv", "send"), None),
            P(("recv", "send"), None),
            P(("recv", "send")),
            P(("recv", "send")),
            P(("recv", "send")),
            P(("recv", "send"), None),
            P(),
            P(),
            P(),
            P(),
            P(),
        ),
        out_specs=(
            P(("recv", "send"), None),
            P(("recv", "send"), None),
            P(("recv", "send"), None),
            P(),
            P(),
            P(),
        ),
        check_vma=False,
    )
```

profile of v0, /device:TPU:0, one launch (start us, length us, event | category | flops | bytes accessed | tf_op | source)
XLA Modules:
  0.0 650.2 jit_solution(7967292514408695948)
XLA Ops:
  7.2 0.0 all-gather.3.cloned.1.call-start
  7.2 0.7 all-gather.3.cloned.1.call-update
  7.9 0.0 all-gather.5.cloned.1.call-start
  7.9 0.7 all-gather.5.cloned.1.call-update
  8.6 0.0 all-reduce.3.cloned.1.call-start
  9.3 0.7 fusion.16
  10.1 18.9 %all-gather.3.cloned.1.call-done = f32[512,512]{1,0:T(8,128)} async-done(((f32[128,512]{1,0:T(8,128)}), f32[512,512]{1,0:T(8,128)}) %all-gather.3.cloned.1.call-update) | async-done | bytes 1048592 | tf_op jit(solution)/shard_map/all_gather | solution.py:58
  29.0 51.5 %all-gather.5.cloned.1.call-done = f32[1024,512]{1,0:T(8,128)} async-done(((f32[128,512]{1,0:T(8,128)}), f32[1024,512]{1,0:T(8,128)}) %all-gather.5.cloned.1.call-update) | async-done | bytes 2097168 | tf_op jit(solution)/shard_map/all_gather | solution.py:59
  80.5 1.1 broadcast.80.clone
  81.6 1.1 broadcast.80
  82.7 1.6 broadcast.81.clone
  84.3 1.6 broadcast.81
  86.0 2.1 broadcast_in_dim.38
  88.0 1.0 copy-done
  89.0 79.1 %while.26 = (s32[]{:T(128)}, f32[1536,512]{1,0:T(8,128)}, f32[512,512]{1,0:T(8,128)}, f32[512]{0:T(512)S(1)}, f32[512]{0:T(512)S(1)}, /*index=5*/f32[512]{0:T(51...) while((s32[]{:T(128)}, f32[1536,512]{1,0:T(8,128)}, ...), condition=%wide.region_11.12_spmd, body=%wide.region_0.11_spmd.sunk | while | flops 4836823040 | bytes 37814700 | solution.py:141
  89.6 0.1 compare_and_fusion.4
  89.7 0.1 compare_and_fusion.5
  89.8 3.2 gather_fusion
  93.0 1.0 broadcast_select_fusion.4
  94.0 0.0 copy-start.2
  94.0 2.9 gather_fusion.1
  96.9 1.1 broadcast_select_fusion.5
  98.1 1.9 convolution_add_fusion.7
  100.0 0.8 fusion.59
  100.8 0.2 multiply_reduce_fusion.6
  101.0 1.2 multiply_reduce_fusion.7
  102.3 1.1 fusion.60
  103.4 1.2 fusion.61
  104.7 3.2 convolution_add_fusion.9
  107.9 4.2 fusion.62
  112.1 4.0 scatter_custom_fusion.11
  116.1 1.8 fusion.63
  117.9 4.7 scatter_custom_fusion.10
  122.6 5.6 convolution_add_fusion.8
  128.9 0.1 compare_and_fusion.4
  129.0 0.1 compare_and_fusion.5
  129.1 3.2 gather_fusion
  132.2 1.0 broadcast_select_fusion.4
  133.3 2.9 gather_fusion.1
  136.2 1.1 broadcast_select_fusion.5
  137.3 1.9 convolution_add_fusion.7
  139.2 0.8 fusion.59
  140.1 0.2 multiply_reduce_fusion.6
  140.3 1.2 multiply_reduce_fusion.7
  141.5 1.1 fusion.60
  142.7 1.2 fusion.61
  143.9 3.2 convolution_add_fusion.9
  147.1 4.2 fusion.62
  151.4 4.0 scatter_custom_fusion.11
  155.3 1.8 fusion.63
  157.1 4.7 scatter_custom_fusion.10
  161.8 5.6 convolution_add_fusion.8
  168.1 0.0 all-reduce.3.cloned.1.call-update
  168.1 0.0 reduce-scatter.3.cloned.1.call-start
  168.2 0.5 reduce-scatter.3.cloned.1.call-update
  168.7 0.0 reduce-scatter.5.cloned.1.call-start
  168.7 0.5 reduce-scatter.5.cloned.1.call-update
  169.3 274.5 %psum.23 = f32[4,512]{1,0:T(4,128)S(1)} all-reduce(f32[4,512]{1,0:T(4,128)S(1)} %pad_maximum_fusion.3), channel_id=1, replica_groups=mesh['recv'=4,'send'=8] {'recv','send'}, use_global_device_ids=true, to_apply=%region_16.17 | all-reduce | flops 2048 | bytes 16384 | tf_op jit(solution)/shard_map/psum | solution.py:148
  443.8 0.6 broadcast_multiply_fusion.5
  444.4 100.4 %all-reduce.3.cloned.1.call-done = (f32[1536,512]{1,0:T(8,128)}, f32[512,512]{1,0:T(8,128)}) async-done(((f32[1536,512]{1,0:T(8,128)}, f32[512,512]{1,0:T(8,128)}), (f32[1536,512]{1,0:T(8,128)}, f32[512,512]{1,0:T(8,128)})) %all-reduce.3.cloned.1.call-update) | async-done | bytes 4194320 | tf_op jit(solution)/shard_map/psum | solution.py:148
  544.8 2.3 broadcast_multiply_fusion.4
  547.1 3.9 broadcast_multiply_fusion.3
  551.0 20.5 %reduce-scatter.3.cloned.1.call-done = f32[128,512]{1,0:T(8,128)} async-done(((f32[512,512]{1,0:T(8,128)}), f32[128,512]{1,0:T(8,128)}) %reduce-scatter.3.cloned.1.call-update) | async-done | bytes 262160 | tf_op jit(solution)/shard_map/reduce_scatter | solution.py:145
  571.6 72.1 %reduce-scatter.5.cloned.1.call-done = f32[128,512]{1,0:T(8,128)} async-done(((f32[1024,512]{1,0:T(8,128)}), f32[128,512]{1,0:T(8,128)}) %reduce-scatter.5.cloned.1.call-update) | async-done | bytes 262160 | tf_op jit(solution)/shard_map/reduce_scatter | solution.py:146
  (47 shorter events, 0.2 us)
Async XLA Ops:
  7.2 21.8 %all-gather.3.cloned.1.call-start = ((), (), s32[]{:S(2)}) async-start(), calls=%async_computation.2 | async-start | bytes 1310720 | tf_op jit(solution)/shard_map/all_gather | solution.py:58
  7.9 72.6 %all-gather.5.cloned.1.call-start = ((), (), s32[]{:S(2)}) async-start(), calls=%async_computation.3 | async-start | bytes 2359296 | tf_op jit(solution)/shard_map/all_gather | solution.py:59
  8.6 536.1 %all-reduce.3.cloned.1.call-start = ((), (), s32[]{:S(2)}) async-start(), calls=%async_computation.6 | async-start | bytes 8388608 | tf_op jit(solution)/shard_map/psum | solution.py:148
  84.3 3.7 copy-start.5
  84.3 3.7 copy-start.6
  84.3 3.7 copy-start.7
  86.0 3.0 copy-start
  94.0 5.9 copy-start.2
  98.1 1.9 copy-start.3
  98.1 1.9 copy-start.4
  98.1 1.9 copy-start.1
  133.3 5.9 copy-start.2
  137.3 1.9 copy-start.3
  137.3 1.9 copy-start.4
  137.3 1.9 copy-start.1
  168.1 403.5 %reduce-scatter.3.cloned.1.call-start = ((), (), s32[]{:S(2)}) async-start(), calls=%async_computation.4 | async-start | bytes 1310720 | tf_op jit(solution)/shard_map/reduce_scatter | solution.py:145
  168.7 475.0 %reduce-scatter.5.cloned.1.call-start = ((), (), s32[]{:S(2)}) async-start(), calls=%async_computation.5 | async-start | bytes 2359296 | tf_op jit(solution)/shard_map/reduce_scatter | solution.py:146
Sparse Core Ops, SparseCore 0:
  9.6 19.4 all-gather.2
  31.1 49.2 all-gather.4
  168.2 376.5 all-reduce.2
  547.8 23.7 reduce-scatter.2
  576.0 67.7 reduce-scatter.4
where the time goes:
time: 654 us; the launch traced here: 650 us
  blocking collectives  275 us (42%)
  waiting for transfers between devices  266 us (41%)
  other arithmetic  38.3 us (6%)
  matrix products  34 us (5%)
  local copies, waits for them, and re-layouts  20.6 us (3%)
  between operations  14.5 us (2%)
    psum x1, blocking collectives, shards(): lax.psum((first_grad, second_grad, small_grads), ('recv', 'send'))  275 us
    psum x1, waiting for transfers between devices, shards(): lax.psum((first_grad, second_grad, small_grads), ('recv', 'send'))  100 us
    reduce_scatter x1, waiting for transfers between devices, shards(): lax.psum_scatter(receiver_acc, 'send', scatter_dimension=0, tiled=True)  72.1 us
    all_gather x1, waiting for transfers between devices, shards(): receiver_table = lax.all_gather(latent, 'send', axis=0, tiled=True)  51.5 us
    reduce_scatter x1, waiting for transfers between devices, shards(): lax.psum_scatter(sender_acc, 'recv', scatter_dimension=0, tiled=True)  20.5 us
    all_gather x1, waiting for transfers between devices, shards(): sender_table = lax.all_gather(latent, 'recv', axis=0, tiled=True)  18.9 us
    dot_general x4, matrix products, outer_sum(): lax.dot_general(left, right, (((0,), (0,)), ((), ())), precision=lax.Prec...  17.7 us
  transfers between devices with their start and end apart: 5, of which 5 were waited for; matrix products, arithmetic and copies ran while one was open for 1% of the time, Pallas kernels for 0%

commit v1 on v0

--- a/solution.py
+++ b/solution.py
@@ -3,6 +3,7 @@
 import jax.numpy as jnp
 from jax import lax
 from jax.sharding import PartitionSpec as P
+from jax.lax import axis_index, axis_size, ppermute
 
 norm_eps = 1e-05
 block_rows = 128
@@ -56,7 +57,19 @@
     send_local = piece_index // send_count * node_rows + senders % node_rows
     live_limit = block_rows * live_blocks[0]
     sender_table = lax.all_gather(latent, "recv", axis=0, tiled=True)
-    receiver_table = lax.all_gather(latent, "send", axis=0, tiled=True)
+    extent = axis_size("send")
+    block_list = [(d, (d + 1) % extent) for d in range(extent)]
+    sides = [(d, (d - 1) % extent) for d in range(extent)]
+    a_next, carry_out = ([latent], [latent])
+    for _ in range(extent // 2):
+        field_out = ppermute(a_next[-1], axis_name="send", perm=block_list)
+        a_next.append(field_out)
+    dev_i = 0
+    while dev_i < (extent - 1) // 2:
+        carry_out.append(ppermute(carry_out[-1], axis_name="send", perm=sides))
+        dev_i = dev_i + 1
+    later = jnp.concatenate([*a_next[::-1], *carry_out[1:]], axis=0)
+    receiver_table = jnp.roll(later, (axis_index("send") - extent // 2) * latent.shape[0], axis=0)
     first_rows = 3 * model_width
 
     def block_work(accs, edge_rows, grad_rows, sender_rows, recv_ids):

time: 654 us -> 627 us (0.959)
  waiting for transfers between devices: 266 us -> 219 us
  starting transfers between devices: 0.19 us -> 26 us
    all_gather x1 -> x0, waiting for transfers between devices: 51.5 us -> none  [shards(): receiver_table = lax.all_gather(latent, 'send', axis=0, tiled=True)]
    ppermute x0 -> x7, starting transfers between devices: none -> 25.8 us  [the longest x3 17.9 us: shards(): carry_out.append(ppermute(carry_out[-1], axis_name='send', perm=sides))]
    ppermute x0 -> x7, waiting for transfers between devices: none -> 23 us  [the longest x4 21.4 us: shards(): field_out = ppermute(a_next[-1], axis_name='send', perm=block_list)]
    all_gather x1, waiting for transfers between devices: 18.9 us -> 0.71 us  [shards(): sender_table = lax.all_gather(latent, 'recv', axis=0, tiled=True)]
  transfers between devices with their start and end apart: 5 -> 11, of which waited for: 5 -> 9; matrix products, arithmetic and copies ran while one was open for 1% -> 2% of each run, Pallas kernels for 0% -> 0%
where the time goes in v1:
time: 627 us; the launch traced here: 624 us
  blocking collectives  269 us (43%)
  waiting for transfers between devices  219 us (35%)
  other arithmetic  38.4 us (6%)
  matrix products  29.9 us (5%)
  starting transfers between devices  26 us (4%)
  local copies, waits for them, and re-layouts  24.4 us (4%)
  between operations  14.6 us (2%)
    psum x1, blocking collectives, shards(): lax.psum((first_grad, second_grad, small_grads), ('recv', 'send'))  269 us
    psum x1, waiting for transfers between devices, shards(): lax.psum((first_grad, second_grad, small_grads), ('recv', 'send'))  101 us
    reduce_scatter x1, waiting for transfers between devices, shards(): lax.psum_scatter(receiver_acc, 'send', scatter_dimension=0, tiled=True)  72.2 us
    ppermute x4, waiting for transfers between devices, shards(): field_out = ppermute(a_next[-1], axis_name='send', perm=block_list)  21.4 us
    reduce_scatter x1, waiting for transfers between devices, shards(): lax.psum_scatter(sender_acc, 'recv', scatter_dimension=0, tiled=True)  20.7 us
    ppermute x3, starting transfers between devices, shards(): carry_out.append(ppermute(carry_out[-1], axis_name='send', perm=sides))  17.9 us
    dot_general x4, matrix products, outer_sum(): lax.dot_general(left, right, (((0,), (0,)), ((), ())), precision=lax.Prec...  13.6 us
  transfers between devices with their start and end apart: 11, of which 9 were waited for; matrix products, arithmetic and copies ran while one was open for 2% of the time, Pallas kernels for 0%

profile of v1, /device:TPU:0, one launch (start us, length us, event | category | flops | bytes accessed | tf_op | source)
XLA Modules:
  0.0 623.8 jit_solution(14411121736397410155)
XLA Ops:
  7.2 3.0 collective-permute-start
  10.2 9.6 %collective-permute-done = f32[128,512]{1,0:T(8,128)S(1)} collective-permute-done((f32[128,512]{1,0:T(8,128)}, f32[128,512]{1,0:T(8,128)S(1)}, u32[]{:S(2)}, u32[]{:S(2)}) %collective-permute-start) | collective-permute-done | bytes 262176 | tf_op jit(solution)/shard_map/ppermute | solution.py:65
  19.8 4.7 collective-permute-start.4
  24.5 6.2 collective-permute-done.1
  30.7 2.5 collective-permute-start.2
  33.2 6.7 %collective-permute-start.5 = (f32[128,512]{1,0:T(8,128)S(1)}, f32[128,512]{1,0:T(8,128)S(1)}, u32[]{:S(2)}, u32[]{:S(2)}) collective-permute-start(f32[128,512]{1,0:T(8,128)S(1)} %collective-permute-done.4), channel_id=1, source_target_pairs={{0,7},{1,0},{2,1},{3,2},{4,3},{5,4},{6,5},{7,6},{8,15},{9,8},{10,9... | collective-permute-start | bytes 786440 | tf_op jit(solution)/shard_map/ppermute | solution.py:69
  39.9 3.3 collective-permute-done.2
  43.2 2.5 collective-permute-start.3
  46.4 0.7 fusion.16
  47.2 6.5 %collective-permute-start.6 = (f32[128,512]{1,0:T(8,128)S(1)}, f32[128,512]{1,0:T(8,128)S(1)}, u32[]{:S(2)}, u32[]{:S(2)}) collective-permute-start(f32[128,512]{1,0:T(8,128)S(1)} %collective-permute-done.5), channel_id=1, source_target_pairs={{0,7},{1,0},{2,1},{3,2},{4,3},{5,4},{6,5},{7,6},{8,15},{9,8},{10,9... | collective-permute-start | bytes 786440 | tf_op jit(solution)/shard_map/ppermute | solution.py:69
  53.6 2.3 collective-permute-done.3
  56.1 1.0 constant_dynamic-update-slice_fusion.11
  57.1 1.6 collective-permute-done.6
  58.9 1.5 constant_dynamic-slice_fusion.1
  60.4 0.7 all-gather.2.cloned.1.call-done
  61.2 1.1 broadcast.81.clone
  62.3 1.1 broadcast.81
  63.4 1.6 broadcast.82.clone
  65.0 1.6 broadcast.82
  66.6 2.1 broadcast_in_dim.38
  68.7 77.4 %while.26 = (s32[]{:T(128)}, f32[1536,512]{1,0:T(8,128)}, f32[512,512]{1,0:T(8,128)}, f32[512]{0:T(512)S(1)}, f32[512]{0:T(512)S(1)}, /*index=5*/f32[512]{0:T(51...) while((s32[]{:T(128)}, f32[1536,512]{1,0:T(8,128)}, ...), condition=%wide.region_11.12_spmd, body=%wide.region_0.11_spmd.sunk | while | flops 4836823040 | bytes 46203364 | solution.py:154
  69.7 3.2 gather_fusion
  72.9 1.0 broadcast_select_fusion.4
  74.0 2.9 gather_fusion.1
  76.8 1.2 broadcast_select_fusion.5
  78.1 1.9 convolution_add_fusion.7
  80.0 0.8 fusion.59
  80.8 0.2 multiply_reduce_fusion.6
  81.0 1.2 multiply_reduce_fusion.7
  82.2 1.1 fusion.60
  83.4 1.2 fusion.61
  84.7 1.2 convolution_add_fusion.9
  85.9 1.0 copy-done.6
  86.8 4.2 fusion.62
  91.1 4.0 scatter_custom_fusion.11
  95.0 1.8 fusion.63
  96.9 4.7 scatter_custom_fusion.10
  101.5 5.6 convolution_add_fusion.8
  108.0 3.2 gather_fusion
  111.2 1.0 broadcast_select_fusion.4
  112.2 2.9 gather_fusion.1
  115.1 1.2 broadcast_select_fusion.5
  116.4 1.9 convolution_add_fusion.7
  118.2 0.8 fusion.59
  119.1 0.2 multiply_reduce_fusion.6
  119.3 1.2 multiply_reduce_fusion.7
  120.5 1.1 fusion.60
  121.7 1.2 fusion.61
  122.9 1.2 convolution_add_fusion.9
  124.1 1.0 copy-done.6
  125.1 4.2 fusion.62
  129.4 4.0 scatter_custom_fusion.11
  133.3 1.8 fusion.63
  135.1 4.7 scatter_custom_fusion.10
  139.8 5.6 convolution_add_fusion.8
  146.1 0.7 reduce-scatter.3.cloned.1.call-update
  146.9 0.5 reduce-scatter.5.cloned.1.call-update
  147.4 268.7 %psum.23 = f32[4,512]{1,0:T(4,128)S(1)} all-reduce(f32[4,512]{1,0:T(4,128)S(1)} %pad_maximum_fusion.3), channel_id=1, replica_groups=mesh['recv'=4,'send'=8] {'recv','send'}, use_global_device_ids=true, to_apply=%region_16.17 | all-reduce | flops 2048 | bytes 16384 | tf_op jit(solution)/shard_map/psum | solution.py:161
  416.1 0.6 broadcast_multiply_fusion.5
  416.7 101.5 %all-reduce.3.cloned.1.call-done = (f32[1536,512]{1,0:T(8,128)}, f32[512,512]{1,0:T(8,128)}) async-done(((f32[1536,512]{1,0:T(8,128)}, f32[512,512]{1,0:T(8,128)}), (f32[1536,512]{1,0:T(8,128)}, f32[512,512]{1,0:T(8,128)})) %all-reduce.3.cloned.1.call-update) | async-done | bytes 4194320 | tf_op jit(solution)/shard_map/psum | solution.py:161
  518.2 2.3 broadcast_multiply_fusion.4
  520.5 3.9 broadcast_multiply_fusion.3
  524.4 20.7 %reduce-scatter.3.cloned.1.call-done = f32[128,512]{1,0:T(8,128)} async-done(((f32[512,512]{1,0:T(8,128)}), f32[128,512]{1,0:T(8,128)}) %reduce-scatter.3.cloned.1.call-update) | async-done | bytes 262160 | tf_op jit(solution)/shard_map/reduce_scatter | solution.py:158
  545.1 72.2 %reduce-scatter.5.cloned.1.call-done = f32[128,512]{1,0:T(8,128)} async-done(((f32[1024,512]{1,0:T(8,128)}), f32[128,512]{1,0:T(8,128)}) %reduce-scatter.5.cloned.1.call-update) | async-done | bytes 262160 | tf_op jit(solution)/shard_map/reduce_scatter | solution.py:159
  (85 shorter events, 1.1 us)
Async XLA Ops:
  7.2 51.6 %copy-start.7 = (f32[128,512]{1,0:T(8,128)S(1)}, f32[128,512]{1,0:T(8,128)}, u32[]{:S(2)}) copy-start(f32[128,512]{1,0:T(8,128)} %param.13) | copy-start | bytes 786436
  7.2 54.0 %all-gather.2.cloned.1.call-start = ((), (), s32[]{:S(2)}) async-start(), calls=%async_computation.2 | async-start | bytes 1310720 | tf_op jit(solution)/shard_map/all_gather | solution.py:59
  7.2 12.6 %collective-permute-start = (f32[128,512]{1,0:T(8,128)}, f32[128,512]{1,0:T(8,128)S(1)}, u32[]{:S(2)}, u32[]{:S(2)}) collective-permute-start(f32[128,512]{1,0:T(8,128)} %param.13), channel_id=1, source_target_pairs={{0,1},{1,2},{2,3},{3,4},{4,5},{5,6},{6,7},{7,0},{8,9},{9,10},{10,1... | collective-permute-start | bytes 786440 | tf_op jit(solution)/shard_map/ppermute | solution.py:65
  19.8 10.9 %collective-permute-start.1 = (f32[128,512]{1,0:T(8,128)S(1)}, f32[128,512]{1,0:T(8,128)S(1)}, u32[]{:S(2)}, u32[]{:S(2)}) collective-permute-start(f32[128,512]{1,0:T(8,128)S(1)} %collective-permute-done), channel_id=1, source_target_pairs={{0,1},{1,2},{2,3},{3,4},{4,5},{5,6},{6,7},{7,0},{8,9},{9,10},{10,1... | collective-permute-start | bytes 786440 | tf_op jit(solution)/shard_map/ppermute | solution.py:65
  19.8 13.4 %collective-permute-start.4 = (f32[128,512]{1,0:T(8,128)}, f32[128,512]{1,0:T(8,128)S(1)}, u32[]{:S(2)}, u32[]{:S(2)}) collective-permute-start(f32[128,512]{1,0:T(8,128)} %param.13), channel_id=1, source_target_pairs={{0,7},{1,0},{2,1},{3,2},{4,3},{5,4},{6,5},{7,6},{8,15},{9,8},{10,9... | collective-permute-start | bytes 786440 | tf_op jit(solution)/shard_map/ppermute | solution.py:69
  30.7 12.5 %collective-permute-start.2 = (f32[128,512]{1,0:T(8,128)S(1)}, f32[128,512]{1,0:T(8,128)S(1)}, u32[]{:S(2)}, u32[]{:S(2)}) collective-permute-start(f32[128,512]{1,0:T(8,128)S(1)} %collective-permute-done.1), channel_id=1, source_target_pairs={{0,1},{1,2},{2,3},{3,4},{4,5},{5,6},{6,7},{7,0},{8,9},{9,10},{10,1... | collective-permute-start | bytes 786440 | tf_op jit(solution)/shard_map/ppermute | solution.py:65
  33.2 14.0 %collective-permute-start.5 = (f32[128,512]{1,0:T(8,128)S(1)}, f32[128,512]{1,0:T(8,128)S(1)}, u32[]{:S(2)}, u32[]{:S(2)}) collective-permute-start(f32[128,512]{1,0:T(8,128)S(1)} %collective-permute-done.4), channel_id=1, source_target_pairs={{0,7},{1,0},{2,1},{3,2},{4,3},{5,4},{6,5},{7,6},{8,15},{9,8},{10,9... | collective-permute-start | bytes 786440 | tf_op jit(solution)/shard_map/ppermute | solution.py:69
  43.2 12.7 %collective-permute-start.3 = (f32[128,512]{1,0:T(8,128)S(1)}, f32[128,512]{1,0:T(8,128)S(1)}, u32[]{:S(2)}, u32[]{:S(2)}) collective-permute-start(f32[128,512]{1,0:T(8,128)S(1)} %collective-permute-done.2), channel_id=1, source_target_pairs={{0,1},{1,2},{2,3},{3,4},{4,5},{5,6},{6,7},{7,0},{8,9},{9,10},{10,1... | collective-permute-start | bytes 786440 | tf_op jit(solution)/shard_map/ppermute | solution.py:65
  45.7 472.4 %all-reduce.3.cloned.1.call-start = ((), (), s32[]{:S(2)}) async-start(), calls=%async_computation.5 | async-start | bytes 8388608 | tf_op jit(solution)/shard_map/psum | solution.py:161
  47.2 11.5 %collective-permute-start.6 = (f32[128,512]{1,0:T(8,128)S(1)}, f32[128,512]{1,0:T(8,128)S(1)}, u32[]{:S(2)}, u32[]{:S(2)}) collective-permute-start(f32[128,512]{1,0:T(8,128)S(1)} %collective-permute-done.5), channel_id=1, source_target_pairs={{0,7},{1,0},{2,1},{3,2},{4,3},{5,4},{6,5},{7,6},{8,15},{9,8},{10,9... | collective-permute-start | bytes 786440 | tf_op jit(solution)/shard_map/ppermute | solution.py:69
  62.3 6.4 %copy-start = (f32[1536,512]{1,0:T(8,128)S(1)}, f32[1536,512]{1,0:T(8,128)}, u32[]{:S(2)}) copy-start(f32[1536,512]{1,0:T(8,128)} %param.19) | copy-start | bytes 9437188
  62.3 6.4 %copy-start.8 = (f32[512]{0:T(512)S(1)}, f32[512]{0:T(512)}, u32[]{:S(2)}) copy-start(f32[512]{0:T(512)} %param.23) | copy-start | bytes 6148
  62.3 6.4 %copy-start.9 = (f32[512]{0:T(512)S(1)}, f32[512]{0:T(512)}, u32[]{:S(2)}) copy-start(f32[512]{0:T(512)} %param.20) | copy-start | bytes 6148
  62.3 6.4 %copy-start.10 = (f32[512]{0:T(512)S(1)}, f32[512]{0:T(512)}, u32[]{:S(2)}) copy-start(f32[512]{0:T(512)} %param.22) | copy-start | bytes 6148
  73.9 6.9 %copy-start.2 = (f32[128,512]{1,0:T(8,128)}, f32[128,512]{1,0:T(8,128)S(1)}, u32[]{:S(2)}) copy-start(f32[128,512]{1,0:T(8,128)S(1)} %broadcast_select_fusion.4) | copy-start | bytes 786436 | tf_op jit(solution)/shard_map/while
  76.8 3.1 copy-start.1
  78.1 6.6 %copy-start.3 = (f32[128,512]{1,0:T(8,128)}, f32[128,512]{1,0:T(8,128)S(1)}, u32[]{:S(2)}) copy-start(f32[128,512]{1,0:T(8,128)S(1)} %get-tuple-element.369) | copy-start | bytes 786436 | tf_op jit(solution)/shard_map/while
  78.1 6.6 %copy-start.4 = (f32[128,512]{1,0:T(8,128)}, f32[128,512]{1,0:T(8,128)S(1)}, u32[]{:S(2)}) copy-start(f32[128,512]{1,0:T(8,128)S(1)} %get-tuple-element.370) | copy-start | bytes 786436 | tf_op jit(solution)/shard_map/while
  78.1 6.6 %copy-start.5 = (f32[512,512]{1,0:T(8,128)S(1)}, f32[512,512]{1,0:T(8,128)}, u32[]{:S(2)}) copy-start(f32[512,512]{1,0:T(8,128)} %get-tuple-element.411) | copy-start | bytes 3145732 | tf_op jit(solution)/shard_map/while
  85.9 1.0 copy-start.6
  112.2 6.9 %copy-start.2 = (f32[128,512]{1,0:T(8,128)}, f32[128,512]{1,0:T(8,128)S(1)}, u32[]{:S(2)}) copy-start(f32[128,512]{1,0:T(8,128)S(1)} %broadcast_select_fusion.4) | copy-start | bytes 786436 | tf_op jit(solution)/shard_map/while
  115.1 3.1 copy-start.1
  116.3 6.6 %copy-start.3 = (f32[128,512]{1,0:T(8,128)}, f32[128,512]{1,0:T(8,128)S(1)}, u32[]{:S(2)}) copy-start(f32[128,512]{1,0:T(8,128)S(1)} %get-tuple-element.369) | copy-start | bytes 786436 | tf_op jit(solution)/shard_map/while
  116.3 6.6 %copy-start.4 = (f32[128,512]{1,0:T(8,128)}, f32[128,512]{1,0:T(8,128)S(1)}, u32[]{:S(2)}) copy-start(f32[128,512]{1,0:T(8,128)S(1)} %get-tuple-element.370) | copy-start | bytes 786436 | tf_op jit(solution)/shard_map/while
  116.3 6.6 %copy-start.5 = (f32[512,512]{1,0:T(8,128)S(1)}, f32[512,512]{1,0:T(8,128)}, u32[]{:S(2)}) copy-start(f32[512,512]{1,0:T(8,128)} %get-tuple-element.411) | copy-start | bytes 3145732 | tf_op jit(solution)/shard_map/while
  124.1 1.0 copy-start.6
  146.1 399.0 %reduce-scatter.3.cloned.1.call-start = ((), (), s32[]{:S(2)}) async-start(), calls=%async_computation.3 | async-start | bytes 1310720 | tf_op jit(solution)/shard_map/reduce_scatter | solution.py:158
  146.8 470.4 %reduce-scatter.5.cloned.1.call-start = ((), (), s32[]{:S(2)}) async-start(), calls=%async_computation.4 | async-start | bytes 2359296 | tf_op jit(solution)/shard_map/reduce_scatter | solution.py:159
Sparse Core Ops, SparseCore 0:
  45.8 15.2 all-gather.1
  146.2 371.8 all-reduce.2
  521.3 23.7 reduce-scatter.2
  549.4 67.7 reduce-scatter.4
